TPU v7x, 32 devices: a whole 2x2x4 slice. The times are simulated.
32 devices in a mesh: cache: 2 (over y), tp: 8 (over z, core), cand: 2 (over x).
Axes of the slice: x: 2, y: 2, z: 4, core: 2. Of those that a mesh axis runs over, the one named last changes fastest.
Arguments:
- prompt_inputs: bfloat16 [1536, 8192], P(('cache', 'cand')), may hold values from -6 to 6
- cand_inputs: bfloat16 [4096, 8192], P(('cache', 'cand'), 'tp'), may hold values from -6 to 6
- norm_gain: float32 [8192], replicated, may hold values from 0.1 to 1.9
- w_query: bfloat16 [8192, 8192], P('cache', 'tp'), may hold values from -0.0625 to 0.0625
- w_key: bfloat16 [8192, 1024], P('cache', 'tp'), may hold values from -0.0625 to 0.0625
- w_value: bfloat16 [8192, 1024], P('cache', 'tp'), may hold values from -0.0625 to 0.0625
- q_bias: float32 [8192], P('tp'), may hold values from -180 to 180
- k_bias: float32 [1024], P('tp'), may hold values from -3 to 8
- v_bias: float32 [1024], P('tp'), may hold values from -4 to 4
- cand_lengths: int32 [16], replicated, may hold values from 32 to 256, as said below
- prefix_ends: int32 [16], replicated, may hold values from 384 to 1536, as said below
Outputs:
- attn_out: bfloat16 [4096, 8192], P(('cache', 'cand'), 'tp')
Inputs may be any that keep to these rules, and one draw needn't show every extreme that they name: `cand_lengths`: at least one candidate has 256 tokens. `prefix_ends`: at least one candidate follows the whole prompt.
All inputs are finite; a program needn't handle non-finite values.
Results may differ from a plain program's by a relative error of at most 0.0075.
The roundings to bfloat16 on the way count: a program that leaves them out, or rounds other values in their place, can miss the bound.
Values may be sent and summed in bfloat16 or wider, within the bound.
A program may use at most 192 MiB of HBM per device.

v0:
```python
import jax
import jax.numpy as jnp
from jax import lax
from jax.sharding import PartitionSpec as P

D = 8192
HEADS = 64
KV_HEADS = 8
HEAD = 128
CANDS = 16
CLEN = 256


ROPE_THETA = 1000000.0
EPSILON = 1e-06


def rotate(tensor, positions):
    half_size = tensor.shape[-1] // 2
    inverse_freq = jnp.power(
        ROPE_THETA, -jnp.arange(half_size, dtype=jnp.float32) * 2.0 / tensor.shape[-1]
    )
    angles = positions.astype(jnp.float32)[:, None] * inverse_freq[None, :]
    cosine = jnp.cos(angles)[:, None, :]
    sine_part = jnp.sin(angles)[:, None, :]
    first_half = tensor[..., :half_size]
    second = tensor[..., half_size:]
    return jnp.concatenate(
        [first_half * cosine - second * sine_part, second * cosine + first_half * sine_part],
        axis=-1,
    )


def row_lookup(row_ids, table):
    chosen = (row_ids // CLEN)[:, None] == jnp.arange(CANDS, dtype=jnp.int32)[None, :]
    return jnp.sum(jnp.where(chosen, table[None, :], 0), axis=1)


def key_visible(row_ids, key_index, prefix_row, prompt_dev, cand_dev):
    unit_rows = prompt_dev + cand_dev
    key_owner = key_index // unit_rows
    key_offset = key_index % unit_rows
    is_prompt = key_offset < prompt_dev
    prompt_pos = key_owner * prompt_dev + key_offset
    cand_row = key_owner * cand_dev + key_offset - prompt_dev
    seen_prompt = prompt_pos[None, :] < prefix_row[:, None]
    seen_cand = ((cand_row // CLEN)[None, :] == (row_ids // CLEN)[:, None]) & (
        cand_row[None, :] <= row_ids[:, None]
    )
    return jnp.where(is_prompt[None, :], seen_prompt, seen_cand)


def attend_block(queries, key_rows, value_rows, visible, running):
    maxima, totals, accumulated = running
    scores = jnp.einsum(
        "rgqd,ngd->rgqn", queries, key_rows, preferred_element_type=jnp.float32
    ) * queries.shape[-1] ** (-0.5)
    visible_four = visible[:, None, None, :]
    new_maxima = jnp.maximum(maxima, jnp.max(jnp.where(visible_four, scores, -1e30), axis=-1))
    weights = jnp.exp(jnp.where(visible_four, scores - new_maxima[..., None], -jnp.inf))
    rescale = jnp.exp(maxima - new_maxima)
    totals = totals * rescale + jnp.sum(weights, axis=-1)
    accumulated = accumulated * rescale[..., None] + jnp.einsum(
        "rgqn,ngd->rgqd",
        weights.astype(jnp.bfloat16),
        value_rows,
        preferred_element_type=jnp.float32,
    )
    return (new_maxima, totals, accumulated)


def block_size(total_rows, unit_rows):
    for multiple in (4, 2, 1):
        if total_rows > multiple * unit_rows and total_rows % (multiple * unit_rows) == 0:
            return multiple * unit_rows
    return total_rows


def per_device(
    prompt_inputs,
    cand_inputs,
    norm_gain,
    w_query,
    w_key,
    w_value,
    q_bias,
    k_bias,
    v_bias,
    cand_lengths,
    prefix_ends,
):
    prompt_dev = prompt_inputs.shape[0]
    cand_dev = cand_inputs.shape[0]
    head_size = HEAD
    kv_local = w_key.shape[1] // head_size
    groups = HEADS // KV_HEADS
    kv_width = kv_local * head_size
    joined = lax.axis_index("cache") * lax.axis_size("cand") + lax.axis_index("cand")
    widened_p = prompt_inputs.astype(jnp.float32)
    normed_p = (
        widened_p
        * lax.rsqrt(jnp.mean(widened_p * widened_p, axis=-1, keepdims=True) + EPSILON)
        * norm_gain
    ).astype(jnp.bfloat16)
    widened_c = cand_inputs.astype(jnp.float32)
    squares = lax.psum(jnp.sum(widened_c * widened_c, axis=-1), "tp")
    part_width = cand_inputs.shape[1]
    gain_part = lax.dynamic_slice_in_dim(norm_gain, lax.axis_index("tp") * part_width, part_width)
    normed_part = (widened_c * lax.rsqrt(squares / D + EPSILON)[:, None] * gain_part).astype(
        jnp.bfloat16
    )
    normed_c = lax.all_gather(normed_part, "tp", axis=1, tiled=True)
    row_ids = joined * cand_dev + jnp.arange(cand_dev, dtype=jnp.int32)
    prefix_row = row_lookup(row_ids, prefix_ends)
    length_row = row_lookup(row_ids, cand_lengths)
    cand_pos = prefix_row + row_ids % CLEN
    prompt_pos = joined * prompt_dev + jnp.arange(prompt_dev, dtype=jnp.int32)
    kv_start = (
        jnp.zeros((prompt_dev, 2 * kv_width), jnp.float32),
        jnp.zeros((cand_dev, 2 * kv_width), jnp.float32),
    )
    initial = (kv_start[0], kv_start[1], jnp.zeros((cand_dev, w_query.shape[1]), jnp.float32))
    piece_key = lax.all_gather(w_key, "cache", axis=0, tiled=True)
    piece_value = lax.all_gather(w_value, "cache", axis=0, tiled=True)
    piece_query = lax.all_gather(w_query, "cache", axis=0, tiled=True)
    key_value = jnp.concatenate([piece_key, piece_value], axis=1)
    kv_prompt = jnp.dot(normed_p, key_value, preferred_element_type=jnp.float32)
    kv_cand = jnp.dot(normed_c, key_value, preferred_element_type=jnp.float32)
    q_cand = jnp.dot(normed_c, piece_query, preferred_element_type=jnp.float32)
    keys_p = rotate(
        (kv_prompt[:, :kv_width] + k_bias).reshape(prompt_dev, kv_local, head_size), prompt_pos
    ).astype(jnp.bfloat16)
    values_p = (
        (kv_prompt[:, kv_width:] + v_bias)
        .astype(jnp.bfloat16)
        .reshape(prompt_dev, kv_local, head_size)
    )
    keys_c = rotate(
        (kv_cand[:, :kv_width] + k_bias).reshape(cand_dev, kv_local, head_size), cand_pos
    ).astype(jnp.bfloat16)
    values_c = (
        (kv_cand[:, kv_width:] + v_bias).astype(jnp.bfloat16).reshape(cand_dev, kv_local, head_size)
    )
    queries = rotate(
        (q_cand + q_bias).reshape(cand_dev, kv_local * groups, head_size), cand_pos
    ).astype(jnp.bfloat16)
    queries = queries.reshape(cand_dev, kv_local, groups, head_size)
    keys_all = jnp.concatenate([keys_p, keys_c], axis=0)
    values_all = jnp.concatenate([values_p, values_c], axis=0)
    unit_rows = prompt_dev + cand_dev
    initial = (
        jnp.full((cand_dev, kv_local, groups), -1e30, jnp.float32),
        jnp.zeros((cand_dev, kv_local, groups), jnp.float32),
        jnp.zeros((cand_dev, kv_local, groups, head_size), jnp.float32),
    )
    piece_key = lax.all_gather(keys_all, ("cache", "cand"), axis=0, tiled=True)
    piece_value = lax.all_gather(values_all, ("cache", "cand"), axis=0, tiled=True)
    piece_rows = piece_key.shape[0]
    block_rows = block_size(piece_rows, unit_rows)

    def advance(turn_index, inner):
        first_row = turn_index * block_rows
        key_block = lax.dynamic_slice_in_dim(piece_key, first_row, block_rows, 0)
        value_block = lax.dynamic_slice_in_dim(piece_value, first_row, block_rows, 0)
        key_index = first_row + jnp.arange(block_rows, dtype=jnp.int32)
        visible = key_visible(row_ids, key_index, prefix_row, prompt_dev, cand_dev)
        return attend_block(queries, key_block, value_block, visible, inner)

    maxima, totals, accumulated = lax.fori_loop(0, piece_rows // block_rows, advance, initial)
    result = accumulated / totals[..., None]
    valid_rows = row_ids % CLEN < length_row
    result = jnp.where(valid_rows[:, None, None, None], result, 0.0).astype(jnp.bfloat16)
    return result.reshape(cand_dev, kv_local * groups * head_size)


def solution(mesh):
    placed = (
        P(("cache", "cand"), None),
        P(("cache", "cand"), "tp"),
        P(),
        P("cache", "tp"),
        P("cache", "tp"),
        P("cache", "tp"),
        P("tp"),
        P("tp"),
        P("tp"),
        P(),
        P(),
    )
    return jax.shard_map(
        per_device,
        mesh=mesh,
        in_specs=placed,
        out_specs=P(("cache", "cand"), "tp"),
        check_vma=False,
    )
```

profile of v0, /device:TPU:0, one launch (start us, length us, event | category | flops | bytes accessed | tf_op | source)
XLA Modules:
  0.0 713.0 jit_solution(11202659701899215689)
XLA Ops:
  6.5 0.0 all-gather.7.cloned.1.call-start
  6.5 0.7 all-gather.7.cloned.1.call-update
  7.3 0.0 all-gather.9.cloned.1.call-start
  7.3 0.7 all-gather.9.cloned.1.call-update
  8.0 0.0 all-gather.11.cloned.1.call-start
  8.1 0.7 dynamic_slice.25
  8.8 2.1 fusion.46
  10.8 18.1 %psum.7 = f32[1024]{0:T(1024)S(1)} all-reduce(f32[1024]{0:T(1024)S(1)} %fusion.46), channel_id=1, replica_groups=mesh['cache'=2,'tp'=8,'cand'=2] {'tp'}, use_global_device_ids=true, to_apply=%region_3.4 | all-reduce | flops 1024 | bytes 8192 | tf_op jit(solution)/shard_map/psum | solution.py:106
  28.9 0.0 copy-done
  28.9 1.9 fusion.48
  30.8 0.0 all-gather.11.cloned.1.call-update
  30.8 0.0 copy-start.7
  30.9 0.0 copy-start.8
  30.9 0.0 all-gather.15.cloned.1.call-start
  30.9 0.5 all-gather.15.cloned.1.call-update
  31.4 0.0 all-gather.13.cloned.1.call-start
  31.5 0.0 copy-done.7
  31.6 0.0 copy-done.8
  31.6 0.7 select_reduce_fusion.1
  32.2 4.1 fusion.39
  36.3 0.7 add_convert_fusion.1
  37.0 7.7 %all-gather.7.cloned.1.call-done = bf16[8192,128]{1,0:T(8,128)(2,1)} async-done(((bf16[4096,128]{1,0:T(8,128)(2,1)}), bf16[8192,128]{1,0:T(8,128)(2,1)}) %all-gather.7.cloned.1.call-update) | async-done | bytes 2097168 | tf_op jit(solution)/shard_map/all_gather | solution.py:123
  44.7 3.1 constant_dynamic-update-slice_fusion.1
  47.9 31.5 %all-gather.9.cloned.1.call-done = bf16[8192,128]{1,0:T(8,128)(2,1)} async-done(((bf16[4096,128]{1,0:T(8,128)(2,1)}), bf16[8192,128]{1,0:T(8,128)(2,1)}) %all-gather.9.cloned.1.call-update) | async-done | bytes 2097168 | tf_op jit(solution)/shard_map/all_gather | solution.py:124
  79.4 3.1 constant_dynamic-update-slice_fusion
  82.5 0.0 copy-done.6
  82.5 6.6 fusion.42
  89.1 0.0 copy-done.4
  89.1 0.0 copy-done.5
  89.1 0.1 fusion.72
  89.2 0.4 fusion.69
  89.7 142.4 %all-gather.11.cloned.1.call-done = bf16[1024,8192]{1,0:T(8,128)(2,1)} async-done(((bf16[1024,1024]{1,0:T(8,128)(2,1)}), bf16[1024,8192]{1,0:T(8,128)(2,1)}) %all-gather.11.cloned.1.call-update) | async-done | bytes 16777232 | tf_op jit(solution)/shard_map/all_gather | solution.py:112
  232.1 10.6 %fusion.80 = f32[1024,256]{0,1:T(8,128)S(1)} fusion(bf16[1024,8192]{1,0:T(8,128)(2,1)} %all-gather.11.cloned.1.call-done, bf16[8192,256]{1,0:T(8,128)(2,1)} %constant_dynamic-update-slice_fusion), kind=kOutput, calls=%fused_computation.138 | convolution fusion | flops 4294967296 | bytes 22020096 | tf_op jit(solution)/shard_map/dot_general | solution.py:128
  242.7 0.0 copy-start.9
  242.7 0.1 fusion.61
  242.8 1.2 fusion.58
  244.0 0.8 maximum_maximum_fusion
  244.8 0.0 all-gather.13.cloned.1.call-update
  244.8 0.2 all-gather.17.cloned.1.call-start
  245.0 0.6 fusion.78
  245.6 1.9 multiply_cosine_fusion
  247.5 0.8 pad_maximum_fusion.1
  248.3 0.0 all-gather.17.cloned.1.call-update
  248.3 182.3 %all-gather.15.cloned.1.call-done = bf16[8192,1024]{1,0:T(8,128)(2,1)} async-done(((bf16[4096,1024]{1,0:T(8,128)(2,1)}), bf16[8192,1024]{1,0:T(8,128)(2,1)}) %all-gather.15.cloned.1.call-update) | async-done | bytes 16777232 | tf_op jit(solution)/shard_map/all_gather | solution.py:125
  430.6 23.4 %convolution_add_fusion = f32[1024,1024]{0,1:T(8,128)S(1)} fusion(bf16[1024,8192]{1,0:T(8,128)(2,1)} %all-gather.11.cloned.1.call-done, bf16[8192,1024]{1,0:T(8,128)(2,1)} %all-gather.15.cloned.1.call-done, f32[1024]{0:T(1024)S(1)} %copy-done.9), kind=kOutput, calls=%fused_computation.76 | convolution fusion | flops 17180917760 | bytes 37752832 | tf_op jit(solution)/shard_map/dot_general | solution.py:129
  454.0 1.7 fusion.79
  455.7 3.8 copy.30
  459.5 2.7 copy.31
  462.2 4.6 fusion.49
  466.9 2.5 pad_maximum_fusion
  469.3 24.2 %all-gather.17.cloned.1.call-done = bf16[5632,1,128]{0,2,1:T(8,128)(2,1)} async-done(((bf16[1408,1,128]{0,2,1:T(8,128)(2,1)}), bf16[5632,1,128]{0,2,1:T(8,128)(2,1)}) %all-gather.17.cloned.1.call-update) | async-done | bytes 1441808 | tf_op jit(solution)/shard_map/all_gather | solution.py:157
  493.5 207.2 %while.23 = (s32[]{:T(128)}, f32[1024,1,8]{0,2,1:T(8,128)S(1)}, f32[1024,1,8]{0,2,1:T(8,128)}, f32[1024,1,8,128]{0,3,2,1:T(8,128)}, s32[1024]{0:T(1024)}, /*inde...) while((s32[]{:T(128)}, f32[1024,1,8]{0,2,1:T(8,128)S(1)}, ...), condition=%wide.region_8.9_spmd.clone.clone.clone, body=%wide.region_5.8_spmd.clone.clone.clone.sunk | while | flops 12082698240 | bytes 301176576 | solution.py:169
  493.7 5.0 and_select_fusion.2
  498.7 33.8 %fusion.97 = (f32[1024,8]{0,1:T(8,128)S(1)}, f32[2816,1024,8]{1,0,2:T(8,128)}) fusion(pred[1024,2816]{0,1:T(8,128)(4,1)S(1)} %and_select_fusion.2, bf16[1024,1,8,128]{3,0,2,1:T(8,128)(2,1)} %get-tuple-element.550, bf16[5632,1,128]{0,2,1:T(8,128)(2,1)} %get-tuple-element.549, s32[]{:T(128)S(6)} %select_n.299), kind=kOutput, calls=%fused_computation.5.clone.1 | convolution fusion | flops 5974777856 | bytes 98009088 | tf_op jit(solution)/shard_map/while/body/eval_jaxpr/rgqd,ngd->rgqn/dot_general | solution.py:55
  532.5 34.8 %bitcast_add_fusion.5 = f32[1024,1,8,128]{0,3,2,1:T(8,128)} fusion(f32[1024,1,8,128]{0,3,2,1:T(8,128)} %get-tuple-element.534, f32[2816,1024,8]{1,0,2:T(8,128)} %get-tuple-element.516, f32[1024,8]{0,1:T(8,128)S(1)} %bitcast.98, pred[1024,2816]{0,1:T(8,128)(4,1)S(1)} %and_select_fusion.2, f32[1024,8]{0,1:T(8,128)S(1)} %get-tuple-element.517, ...), kind=kOutput, calls=%fused_computation.14.clone.1 | convolution fusion | flops 6001000448 | bytes 104333320 | tf_op jit(solution)/shard_map/while/body/eval_jaxpr/rgqn,ngd->rgqd/dot_general | solution.py:63
  567.3 28.8 %fusion.99 = f32[1024,8]{0,1:T(8,128)S(1)} fusion(f32[2816,1024,8]{1,0,2:T(8,128)} %get-tuple-element.516, f32[1024,8]{0,1:T(8,128)S(1)} %bitcast.99, pred[1024,2816]{0,1:T(8,128)(4,1)S(1)} %and_select_fusion.2), kind=kLoop, calls=%fused_computation.9.clone.1 | loop fusion | flops 92266496 | bytes 95223808 | tf_op jit(solution)/shard_map/while/body/eval_jaxpr/reduce_sum | solution.py:62
  596.2 0.6 copy-done.2
  597.0 5.0 and_select_fusion.2
  602.0 33.8 %fusion.97 = (f32[1024,8]{0,1:T(8,128)S(1)}, f32[2816,1024,8]{1,0,2:T(8,128)}) fusion(pred[1024,2816]{0,1:T(8,128)(4,1)S(1)} %and_select_fusion.2, bf16[1024,1,8,128]{3,0,2,1:T(8,128)(2,1)} %get-tuple-element.550, bf16[5632,1,128]{0,2,1:T(8,128)(2,1)} %get-tuple-element.549, s32[]{:T(128)S(6)} %select_n.299), kind=kOutput, calls=%fused_computation.5.clone.1 | convolution fusion | flops 5974777856 | bytes 98009088 | tf_op jit(solution)/shard_map/while/body/eval_jaxpr/rgqd,ngd->rgqn/dot_general | solution.py:55
  635.8 35.4 %bitcast_add_fusion.5 = f32[1024,1,8,128]{0,3,2,1:T(8,128)} fusion(f32[1024,1,8,128]{0,3,2,1:T(8,128)} %get-tuple-element.534, f32[2816,1024,8]{1,0,2:T(8,128)} %get-tuple-element.516, f32[1024,8]{0,1:T(8,128)S(1)} %bitcast.98, pred[1024,2816]{0,1:T(8,128)(4,1)S(1)} %and_select_fusion.2, f32[1024,8]{0,1:T(8,128)S(1)} %get-tuple-element.517, ...), kind=kOutput, calls=%fused_computation.14.clone.1 | convolution fusion | flops 6001000448 | bytes 104333320 | tf_op jit(solution)/shard_map/while/body/eval_jaxpr/rgqn,ngd->rgqd/dot_general | solution.py:63
  671.2 28.8 %fusion.99 = f32[1024,8]{0,1:T(8,128)S(1)} fusion(f32[2816,1024,8]{1,0,2:T(8,128)} %get-tuple-element.516, f32[1024,8]{0,1:T(8,128)S(1)} %bitcast.99, pred[1024,2816]{0,1:T(8,128)(4,1)S(1)} %and_select_fusion.2), kind=kLoop, calls=%fused_computation.9.clone.1 | loop fusion | flops 92266496 | bytes 95223808 | tf_op jit(solution)/shard_map/while/body/eval_jaxpr/reduce_sum | solution.py:62
  700.1 0.6 copy-done.2
  700.7 2.8 select_convert_fusion
  703.6 2.6 copy.28
  (40 shorter events, 0.4 us)
Async XLA Ops:
  6.5 22.4 %copy-start = (bf16[1024,1024]{1,0:T(8,128)(2,1)S(1)}, bf16[1024,1024]{1,0:T(8,128)(2,1)}, u32[]{:S(2)}) copy-start(bf16[1024,1024]{1,0:T(8,128)(2,1)} %param.14) | copy-start | bytes 6291460
  6.5 38.2 %all-gather.7.cloned.1.call-start = ((), (), s32[]{:S(2)}) async-start(), calls=%async_computation | async-start | bytes 3145728 | tf_op jit(solution)/shard_map/all_gather | solution.py:123
  7.3 72.1 %all-gather.9.cloned.1.call-start = ((), (), s32[]{:S(2)}) async-start(), calls=%async_computation.1 | async-start | bytes 3145728 | tf_op jit(solution)/shard_map/all_gather | solution.py:124
  8.0 224.1 %all-gather.11.cloned.1.call-start = ((), (), s32[]{:S(2)}) async-start(), calls=%async_computation.2 | async-start | bytes 18874368 | tf_op jit(solution)/shard_map/all_gather | solution.py:112
  30.8 0.7 copy-start.7
  30.9 0.7 copy-start.8
  30.9 399.7 %all-gather.15.cloned.1.call-start = ((), (), s32[]{:S(2)}) async-start(), calls=%async_computation.4 | async-start | bytes 25165824 | tf_op jit(solution)/shard_map/all_gather | solution.py:125
  31.4 437.9 %all-gather.13.cloned.1.call-start = ((), (), s32[]{:S(2)}) async-start(), calls=%async_computation.3 | async-start | bytes 1802240 | tf_op jit(solution)/shard_map/all_gather | solution.py:156
  37.0 45.4 %copy-start.6 = (f32[8192]{0:T(1024)S(1)}, f32[8192]{0:T(1024)}, u32[]{:S(2)}) copy-start(f32[8192]{0:T(1024)} %param.15) | copy-start | bytes 98308
  82.5 6.6 copy-start.4
  82.5 6.6 copy-start.5
  242.7 187.9 %copy-start.9 = (f32[1024]{0:T(1024)S(1)}, f32[1024]{0:T(1024)}, u32[]{:S(2)}) copy-start(f32[1024]{0:T(1024)} %param.19) | copy-start | bytes 12292
  244.8 248.8 %all-gather.17.cloned.1.call-start = ((), (), s32[]{:S(2)}) async-start(), calls=%async_computation.5 | async-start | bytes 1802240 | tf_op jit(solution)/shard_map/all_gather | solution.py:157
  493.5 207.2 %copy-start.3 = (pred[1024]{0:T(1024)(128)(4,1)S(1)}, pred[1024]{0:T(1024)(128)(4,1)}, u32[]{:S(2)}) copy-start(pred[1024]{0:T(1024)(128)(4,1)} %fusion.78) | copy-start | bytes 3076
  567.3 28.9 %copy-start.1 = (f32[1024,1,8]{0,2,1:T(8,128)S(1)}, f32[1024,1,8]{0,2,1:T(8,128)}, u32[]{:S(2)}) copy-start(f32[1024,1,8]{0,2,1:T(8,128)} %get-tuple-element.533) | copy-start | bytes 98308 | tf_op jit(solution)/shard_map/while
  596.2 0.6 copy-start.2
  671.2 28.9 %copy-start.1 = (f32[1024,1,8]{0,2,1:T(8,128)S(1)}, f32[1024,1,8]{0,2,1:T(8,128)}, u32[]{:S(2)}) copy-start(f32[1024,1,8]{0,2,1:T(8,128)} %get-tuple-element.533) | copy-start | bytes 98308 | tf_op jit(solution)/shard_map/while
  700.1 0.6 copy-start.2
Sparse Core Ops, SparseCore 0:
  8.9 35.8 all-gather.6
  46.3 33.0 all-gather.8
  81.0 151.0 all-gather.10
  233.5 197.0 all-gather.14
  432.3 29.7 all-gather.12
  463.7 29.7 all-gather.16
where the time goes:
time: 714 us; the launch traced here: 713 us
  waiting for transfers between devices  390 us (55%)
  matrix products  178 us (25%)
  other arithmetic  93.2 us (13%)
  local copies, waits for them, and re-layouts  18.9 us (3%)
  blocking collectives  18.1 us (3%)
  between operations  13.7 us (2%)
    all_gather x1, waiting for transfers between devices, per_device(): piece_query = lax.all_gather(w_query, 'cache', axis=0, tiled=True)  182 us
    all_gather x1, waiting for transfers between devices, per_device(): normed_c = lax.all_gather(normed_part, 'tp', axis=1, tiled=True)  142 us
    dot_general x2, matrix products, attend_block(): jnp.einsum('rgqn,ngd->rgqd', weights.astype(jnp.bfloat16), value_rows, pr...  70.2 us
    dot_general x2, matrix products, attend_block(): jnp.einsum('rgqd,ngd->rgqn', queries, key_rows, preferred_element_type=jn...  67.6 us
    reduce_sum x2, other arithmetic, attend_block(): totals = totals * rescale + jnp.sum(weights, axis=-1)  57.7 us
    all_gather x1, waiting for transfers between devices, per_device(): piece_value = lax.all_gather(w_value, 'cache', axis=0, tiled=True)  31.5 us
    all_gather x1, waiting for transfers between devices, per_device(): lax.all_gather(values_all, ('cache', 'cand'), axis=0, tiled=True)  24.2 us
    dot_general x1, matrix products, per_device(): q_cand = jnp.dot(normed_c, piece_query, preferred_element_type=jnp.float32)  23.4 us
  transfers between devices with their start and end apart: 6, of which 5 were waited for; matrix products, arithmetic and copies ran while one was open for 11% of the time, Pallas kernels for 0%

commit v1 on v0

v1 whole, which is shorter than its diff:
```python
import functools
import math

import jax
import jax.numpy as jnp
from jax import lax
from jax.experimental import pallas as pl
from jax.experimental.pallas import tpu as pltpu
from jax.sharding import PartitionSpec as P

D = 8192
HEADS = 64
KV_HEADS = 8
HEAD = 128
CANDS = 16
CLEN = 256


ROPE_THETA = 1000000.0
EPSILON = 1e-06


def rotate(tensor, positions):
    half_size = tensor.shape[-1] // 2
    inverse_freq = jnp.power(
        ROPE_THETA, -jnp.arange(half_size, dtype=jnp.float32) * 2.0 / tensor.shape[-1]
    )
    angles = positions.astype(jnp.float32)[:, None] * inverse_freq[None, :]
    cosine = jnp.cos(angles)[:, None, :]
    sine_part = jnp.sin(angles)[:, None, :]
    first_half = tensor[..., :half_size]
    second = tensor[..., half_size:]
    return jnp.concatenate(
        [first_half * cosine - second * sine_part, second * cosine + first_half * sine_part],
        axis=-1,
    )


def row_lookup(row_ids, table):
    chosen = (row_ids // CLEN)[:, None] == jnp.arange(CANDS, dtype=jnp.int32)[None, :]
    return jnp.sum(jnp.where(chosen, table[None, :], 0), axis=1)


def attend_kernel(
    prefix_ref, length_ref, offset_ref, q_ref, kvp_ref, kvc_ref, out_ref, *, heads, chunk, scale
):
    cand = pl.program_id(0)
    prefix = prefix_ref[cand]
    length = length_ref[cand]
    offset = offset_ref[cand]
    rows = q_ref.shape[0]
    contract = (((1,), (1,)), ((), ()))

    def scores_of(head, key_rows):
        return (
            lax.dot_general(
                q_ref[:, head * HEAD : (head + 1) * HEAD],
                key_rows,
                contract,
                preferred_element_type=jnp.float32,
            )
            * scale
        )

    def weighted(probabilities, value_rows):
        return jnp.dot(
            probabilities.astype(jnp.bfloat16), value_rows, preferred_element_type=jnp.float32
        )

    own_shape = (rows, kvc_ref.shape[0])
    causal = lax.broadcasted_iota(jnp.int32, own_shape, 1) <= offset + lax.broadcasted_iota(
        jnp.int32, own_shape, 0
    )
    state = []
    for head in range(heads):
        scores = jnp.where(causal, scores_of(head, kvc_ref[:, :HEAD]), -1e30)
        maxima = jnp.max(scores, axis=1, keepdims=True)
        probabilities = jnp.exp2(scores - maxima)
        totals = jnp.sum(probabilities, axis=1, keepdims=True)
        state += [maxima, totals, weighted(probabilities, kvc_ref[:, HEAD:])]

    def advance(turn, running):
        first = pl.multiple_of(turn * chunk, chunk)
        key_rows = kvp_ref[pl.ds(first, chunk), :HEAD]
        value_rows = kvp_ref[pl.ds(first, chunk), HEAD:]
        seen = first + lax.broadcasted_iota(jnp.int32, (rows, chunk), 1) < prefix
        following = []
        for head in range(heads):
            maxima, totals, accumulated = running[3 * head : 3 * head + 3]
            scores = jnp.where(seen, scores_of(head, key_rows), -1e30)
            new_maxima = jnp.maximum(maxima, jnp.max(scores, axis=1, keepdims=True))
            probabilities = jnp.exp2(scores - new_maxima)
            rescale = jnp.exp2(maxima - new_maxima)
            totals = totals * rescale + jnp.sum(probabilities, axis=1, keepdims=True)
            accumulated = accumulated * rescale + weighted(probabilities, value_rows)
            following += [new_maxima, totals, accumulated]
        return tuple(following)

    state = lax.fori_loop(0, (prefix + chunk - 1) // chunk, advance, tuple(state))
    valid = offset + lax.broadcasted_iota(jnp.int32, (rows, HEAD), 0) < length
    for head in range(heads):
        result = state[3 * head + 2] / state[3 * head + 1]
        out_ref[:, head * HEAD : (head + 1) * HEAD] = jnp.where(valid, result, 0.0).astype(
            jnp.bfloat16
        )


def attend(prefixes, lengths, offsets, queries, kv_prompt, kv_cand, kv_local, groups):
    tiles = prefixes.shape[0]
    rows = queries.shape[0] // tiles
    prompt = kv_prompt.shape[0]
    chunk = next(size for size in (512, 256, 128, prompt) if prompt % size == 0)
    heads = 2 if groups % 2 == 0 else 1
    turns = groups // heads
    return pl.pallas_call(
        functools.partial(
            attend_kernel, heads=heads, chunk=chunk, scale=HEAD ** (-0.5) * math.log2(math.e)
        ),
        grid_spec=pltpu.PrefetchScalarGridSpec(
            num_scalar_prefetch=3,
            grid=(tiles, kv_local, turns),
            in_specs=[
                pl.BlockSpec((rows, heads * HEAD), lambda c, k, t, *_: (c, k * turns + t)),
                pl.BlockSpec((prompt, 2 * HEAD), lambda c, k, t, *_: (0, k)),
                pl.BlockSpec((CLEN, 2 * HEAD), lambda c, k, t, *_: (c, k)),
            ],
            out_specs=pl.BlockSpec((rows, heads * HEAD), lambda c, k, t, *_: (c, k * turns + t)),
        ),
        out_shape=jax.ShapeDtypeStruct(queries.shape, jnp.bfloat16),
        cost_estimate=pl.CostEstimate(
            flops=4 * queries.size * (prompt + CLEN),
            bytes_accessed=4 * queries.size,
            transcendentals=queries.size // HEAD * (prompt + CLEN),
        ),
        compiler_params=pltpu.CompilerParams(vmem_limit_bytes=60 * 1024 * 1024),
    )(prefixes, lengths, offsets, queries, kv_prompt, kv_cand)


def query_product(normed, w_query):
    caches = lax.axis_size("cache")
    cands = lax.axis_size("cand")
    depth = w_query.shape[0]
    if caches != 2 or cands != 2 or depth % 4 != 0:
        return jnp.dot(
            normed,
            lax.all_gather(w_query, "cache", axis=0, tiled=True),
            preferred_element_type=jnp.float32,
        )
    mine = lax.axis_index("cache")
    side = lax.axis_index("cand")
    part = depth // 4
    swap = [(0, 1), (1, 0)]
    direct = [
        lax.ppermute(
            lax.dynamic_slice_in_dim(w_query, (2 * side + turn) * part, part), "cache", swap
        )
        for turn in range(2)
    ]
    relayed = [lax.ppermute(piece, "cand", swap) for piece in direct]

    def product(first, weights):
        columns = lax.dynamic_slice_in_dim(normed, first, weights.shape[0], 1)
        return jnp.dot(columns, weights, preferred_element_type=jnp.float32)

    total = product(mine * depth, w_query)
    other = (1 - mine) * depth
    for turn in range(2):
        total = total + product(other + (2 * side + turn) * part, direct[turn])
    for turn in range(2):
        total = total + product(other + (2 * (1 - side) + turn) * part, relayed[turn])
    return total


def per_device(
    prompt_inputs,
    cand_inputs,
    norm_gain,
    w_query,
    w_key,
    w_value,
    q_bias,
    k_bias,
    v_bias,
    cand_lengths,
    prefix_ends,
):
    prompt_dev = prompt_inputs.shape[0]
    cand_dev = cand_inputs.shape[0]
    head_size = HEAD
    kv_local = w_key.shape[1] // head_size
    groups = HEADS // KV_HEADS
    kv_width = kv_local * head_size
    joined = lax.axis_index("cache") * lax.axis_size("cand") + lax.axis_index("cand")
    widened_p = prompt_inputs.astype(jnp.float32)
    normed_p = (
        widened_p
        * lax.rsqrt(jnp.mean(widened_p * widened_p, axis=-1, keepdims=True) + EPSILON)
        * norm_gain
    ).astype(jnp.bfloat16)
    widened_c = cand_inputs.astype(jnp.float32)
    squares = lax.psum(jnp.sum(widened_c * widened_c, axis=-1), "tp")
    part_width = cand_inputs.shape[1]
    gain_part = lax.dynamic_slice_in_dim(norm_gain, lax.axis_index("tp") * part_width, part_width)
    normed_part = (widened_c * lax.rsqrt(squares / D + EPSILON)[:, None] * gain_part).astype(
        jnp.bfloat16
    )
    normed_c = lax.all_gather(normed_part, "tp", axis=1, tiled=True)
    row_ids = joined * cand_dev + jnp.arange(cand_dev, dtype=jnp.int32)
    prefix_row = row_lookup(row_ids, prefix_ends)
    cand_pos = prefix_row + row_ids % CLEN
    prompt_pos = joined * prompt_dev + jnp.arange(prompt_dev, dtype=jnp.int32)
    key_value = jnp.concatenate([w_key, w_value], axis=1)
    key_value = lax.all_gather(key_value, "cache", axis=0, tiled=True)
    kv_prompt = jnp.dot(normed_p, key_value, preferred_element_type=jnp.float32)

    def keys_values(product, positions):
        rows = product.shape[0]
        keys = rotate(
            (product[:, :kv_width] + k_bias).reshape(rows, kv_local, head_size), positions
        ).astype(jnp.bfloat16)
        values = (product[:, kv_width:] + v_bias).astype(jnp.bfloat16)
        values = values.reshape(rows, kv_local, head_size)
        return jnp.concatenate([keys, values], axis=2).reshape(rows, 2 * kv_width)

    kv_p = lax.all_gather(
        keys_values(kv_prompt, prompt_pos), ("cache", "cand"), axis=0, tiled=True
    )
    q_cand = query_product(normed_c, w_query)
    kv_c = keys_values(jnp.dot(normed_c, key_value, preferred_element_type=jnp.float32), cand_pos)
    queries = rotate(
        (q_cand + q_bias).reshape(cand_dev, kv_local * groups, head_size), cand_pos
    ).astype(jnp.bfloat16)
    tile_rows = min(cand_dev, CLEN)
    tile_first = joined * cand_dev + tile_rows * jnp.arange(cand_dev // tile_rows, dtype=jnp.int32)
    prefixes = row_lookup(tile_first, prefix_ends)
    lengths = row_lookup(tile_first, cand_lengths)
    offsets = tile_first % CLEN
    if cand_dev < CLEN:
        kv_c = lax.all_gather(kv_c, ("cache", "cand"), axis=0, tiled=True)
        kv_c = lax.dynamic_slice_in_dim(kv_c, joined * cand_dev // CLEN * CLEN, CLEN)
    return attend(
        prefixes,
        lengths,
        offsets,
        queries.reshape(cand_dev, kv_local * groups * head_size),
        kv_p,
        kv_c,
        kv_local,
        groups,
    )


def solution(mesh):
    placed = (
        P(("cache", "cand"), None),
        P(("cache", "cand"), "tp"),
        P(),
        P("cache", "tp"),
        P("cache", "tp"),
        P("cache", "tp"),
        P("tp"),
        P("tp"),
        P("tp"),
        P(),
        P(),
    )
    return jax.shard_map(
        per_device,
        mesh=mesh,
        in_specs=placed,
        out_specs=P(("cache", "cand"), "tp"),
        check_vma=False,
    )
```

time: 714 us -> 382 us (0.54)
  waiting for transfers between devices: 390 us -> 159 us
  matrix products: 178 us -> 53.5 us
  other arithmetic: 93.2 us -> 22.8 us
  blocking collectives: 18.1 us -> 64.2 us
  Pallas kernels: 0 us -> 46 us
    all_gather x5 -> x1, waiting for transfers between devices: 246 us -> 0.01 us  [per_device(): key_value = lax.all_gather(key_value, 'cache', axis=0, tiled=True)]
    dot_general x6, matrix products: 172 us -> 47.6 us  [the longest x5 39.4 us: product(): return jnp.dot(columns, weights, preferred_element_type=jnp.float32)]
    ppermute x0 -> x4, waiting for transfers between devices: none -> 114 us  [the longest x2 114 us: query_product(): lax.ppermute(lax.dynamic_slice_in_dim(w_query, (2 * side + turn) * part,...]
    all_gather x1, waiting for transfers between devices: 142 us -> 45.1 us  [per_device(): normed_c = lax.all_gather(normed_part, 'tp', axis=1, tiled=True)]
    reduce_sum x2 -> x0, other arithmetic: 57.7 us -> none  [attend_block(): totals = totals * rescale + jnp.sum(weights, axis=-1)]
    all_gather x0 -> x1, blocking collectives: none -> 46.1 us  [per_device(): lax.all_gather(keys_values(kv_prompt, prompt_pos), ('cache', 'cand'), axi...]
    pallas_call x0 -> x1, Pallas kernels: none -> 46 us  [attend(): pl.pallas_call(functools.partial(attend_kernel, heads=heads, chunk=chunk,...]
    select_n x6 -> x1, other arithmetic: 10.1 us -> 0.6 us  [per_device(): offsets = tile_first % CLEN]
  transfers between devices with their start and end apart: 6 -> 6, of which waited for: 5 -> 3; matrix products, arithmetic and copies ran while one was open for 11% -> 14% of each run, Pallas kernels for 0% -> 0%
where the time goes in v1:
time: 382 us; the launch traced here: 378 us
  waiting for transfers between devices  159 us (42%)
  blocking collectives  64.2 us (17%)
  matrix products  53.5 us (14%)
  Pallas kernels  46 us (12%)
  other arithmetic  22.8 us (6%)
  local copies, waits for them, and re-layouts  14.3 us (4%)
  between operations  13.6 us (4%)
  starting transfers between devices  5.01 us (1%)
    ppermute x2, waiting for transfers between devices, query_product(): lax.ppermute(lax.dynamic_slice_in_dim(w_query, (2 * side + turn) * part,...  114 us
    all_gather x1, blocking collectives, per_device(): lax.all_gather(keys_values(kv_prompt, prompt_pos), ('cache', 'cand'), axi...  46.1 us
    pallas_call x1, Pallas kernels, attend(): pl.pallas_call(functools.partial(attend_kernel, heads=heads, chunk=chunk,...  46 us
    all_gather x1, waiting for transfers between devices, per_device(): normed_c = lax.all_gather(normed_part, 'tp', axis=1, tiled=True)  45.1 us
    dot_general x5, matrix products, product(): return jnp.dot(columns, weights, preferred_element_type=jnp.float32)  39.4 us
    psum x1, blocking collectives, per_device(): squares = lax.psum(jnp.sum(widened_c * widened_c, axis=-1), 'tp')  18.1 us
    unnamed x19, local copies, waits for them, and re-layouts  8.61 us
    dot_general x1, matrix products, per_device(): jnp.dot(normed_c, key_value, preferred_element_type=jnp.float32)  8.16 us
  transfers between devices with their start and end apart: 6, of which 3 were waited for; matrix products, arithmetic and copies ran while one was open for 14% of the time, Pallas kernels for 0%

profile of v1, /device:TPU:0, one launch (start us, length us, event | category | flops | bytes accessed | tf_op | source)
XLA Modules:
  0.0 378.4 jit_solution(3573306632877436179)
XLA Ops:
  6.5 0.0 copy-start.6
  6.5 0.0 copy-start
  6.5 0.0 all-gather.6.cloned.1.call-start
  6.5 3.3 pad_maximum_fusion.1
  9.8 0.0 all-gather.6.cloned.1.call-update
  9.8 0.0 all-gather.4.cloned.1.call-start
  9.9 0.0 copy-done.6
  9.9 0.0 copy-done
  9.9 0.5 fusion.9
  10.4 18.1 %psum.7 = f32[1024]{0:T(1024)S(1)} all-reduce(f32[1024]{0:T(1024)S(1)} %fusion.9), channel_id=1, replica_groups=mesh['cache'=2,'tp'=8,'cand'=2] {'tp'}, use_global_device_ids=true, to_apply=%region_3.4 | all-reduce | flops 1024 | bytes 8192 | tf_op jit(solution)/shard_map/psum | solution.py:201
  28.5 1.9 fusion.11
  30.4 0.0 all-gather.4.cloned.1.call-update
  30.4 0.0 copy-start.2
  30.4 0.0 copy-start.5
  30.4 4.0 %constant_dynamic-slice_fusion = (bf16[1024,1024]{1,0:T(8,128)(2,1)S(1)}, bf16[1024,1024]{1,0:T(8,128)(2,1)}) fusion(bf16[4096,1024]{1,0:T(8,128)(2,1)} %param.14, s32[]{:T(128)S(6)} %select_n.80, s32[]{:T(128)S(6)} %select_n.78), kind=kLoop, calls=%fused_computation.89 | loop fusion | bytes 8388616 | tf_op jit(solution)/shard_map/dynamic_slice | solution.py:155
  34.4 1.5 collective-permute-start
  36.0 0.5 collective-permute-start.1
  36.5 0.6 and_select_fusion.offset_ref
  37.1 0.0 copy-done.2
  37.1 0.0 copy-done.5
  37.1 0.8 select_reduce_fusion.1
  37.9 0.1 select_reduce_fusion
  38.0 4.1 %fusion = f32[384]{0:T(512)S(1)} fusion(bf16[384,8192]{1,0:T(8,128)(2,1)} %param.11), kind=kLoop, calls=%fused_computation.2 | loop fusion | flops 9436800 | bytes 6292992 | tf_op jit(solution)/shard_map/reduce_sum | solution.py:197
  42.1 1.9 multiply_cosine_fusion.1
  44.0 0.0 copy-start.3
  44.0 0.0 copy-start.4
  44.0 71.5 %collective-permute-done = bf16[1024,1024]{1,0:T(8,128)(2,1)} collective-permute-done((bf16[1024,1024]{1,0:T(8,128)(2,1)}, bf16[1024,1024]{1,0:T(8,128)(2,1)}, u32[]{:S(2)}, u32[]{:S(2)}) %collective-permute-start) | collective-permute-done | bytes 2097184 | tf_op jit(solution)/shard_map/ppermute | solution.py:154
  115.5 1.5 collective-permute-start.2
  117.0 42.2 %collective-permute-done.1 = bf16[1024,1024]{1,0:T(8,128)(2,1)} collective-permute-done((bf16[1024,1024]{1,0:T(8,128)(2,1)S(1)}, bf16[1024,1024]{1,0:T(8,128)(2,1)}, u32[]{:S(2)}, u32[]{:S(2)}) %collective-permute-start.1) | collective-permute-done | bytes 2097184 | tf_op jit(solution)/shard_map/ppermute | solution.py:154
  159.2 1.5 collective-permute-start.3
  160.6 0.0 all-gather.6.cloned.1.call-done
  160.6 5.9 %fusion.5 = f32[384,256]{1,0:T(8,128)S(1)} fusion(bf16[8192,256]{1,0:T(8,128)(2,1)} %all-gather.6.cloned.1.call-done, bf16[384,8192]{1,0:T(8,128)(2,1)} %param.11, f32[8192]{0:T(1024)S(1)} %copy-done.6, f32[384]{0:T(512)S(1)} %add_rsqrt_fusion.1), kind=kOutput, calls=%fused_computation.7 | convolution fusion | flops 1623195648 | bytes 10913280 | tf_op jit(solution)/shard_map/dot_general | solution.py:214
  166.6 0.0 copy-done.3
  166.6 0.0 copy-done.4
  166.6 0.8 fusion.38
  167.5 0.1 pad_maximum_fusion.2
  167.6 46.1 %all-gather = bf16[1536,1,256]{2,0,1:T(8,128)(2,1)} all-gather(bf16[384,1,256]{2,0,1:T(8,128)(2,1)S(1)} %pad_maximum_fusion.2), channel_id=2, replica_groups=mesh['cache'=2,'tp'=8,'cand'=2] {'cache','cand'}, dimensions={0}, use_global_device_ids=true | all-gather | bytes 983040 | tf_op jit(solution)/shard_map/all_gather | solution.py:225
  213.7 45.1 %all-gather.4.cloned.1.call-done = bf16[1024,8192]{1,0:T(8,128)(2,1)} async-done(((bf16[1024,1024]{1,0:T(8,128)(2,1)}), bf16[1024,8192]{1,0:T(8,128)(2,1)}) %all-gather.4.cloned.1.call-update) | async-done | bytes 16777232 | tf_op jit(solution)/shard_map/all_gather | solution.py:207
  258.8 4.7 %fusion.16 = f32[1024,1024]{0,1:T(8,128)S(1)} fusion(bf16[1024,1024]{1,0:T(8,128)(2,1)} %collective-permute-done.1, bf16[1024,8192]{1,0:T(8,128)(2,1)} %all-gather.4.cloned.1.call-done, s32[]{:T(128)S(6)} %select_n.79), kind=kOutput, calls=%fused_computation.25 | convolution fusion | flops 2147483648 | bytes 8388612 | tf_op jit(solution)/shard_map/dot_general | solution.py:163
  263.5 4.7 %fusion.18 = f32[1024,1024]{0,1:T(8,128)S(1)} fusion(bf16[1024,1024]{1,0:T(8,128)(2,1)} %collective-permute-done, bf16[1024,8192]{1,0:T(8,128)(2,1)} %all-gather.4.cloned.1.call-done, s32[]{:T(128)S(6)} %select_n.77), kind=kOutput, calls=%fused_computation.27 | convolution fusion | flops 2147483648 | bytes 8388612 | tf_op jit(solution)/shard_map/dot_general | solution.py:163
  268.2 0.0 collective-permute-done.2
  268.2 6.6 %fusion.14 = f32[1024,1024]{0,1:T(8,128)} fusion(bf16[1024,1024]{1,0:T(8,128)(2,1)} %collective-permute-done.2, bf16[1024,8192]{1,0:T(8,128)(2,1)} %all-gather.4.cloned.1.call-done, s32[]{:T(128)S(6)} %select_n.81), kind=kOutput, calls=%fused_computation.23 | convolution fusion | flops 2147483648 | bytes 8388612 | tf_op jit(solution)/shard_map/dot_general | solution.py:163
  274.8 0.0 copy-start.1
  274.8 15.1 %fusion.3 = f32[1024,1024]{0,1:T(8,128)} fusion(bf16[4096,1024]{1,0:T(8,128)(2,1)} %param.14, bf16[1024,8192]{1,0:T(8,128)(2,1)} %all-gather.4.cloned.1.call-done, s32[]{:T(128)S(6)} %select_n.76), kind=kOutput, calls=%fused_computation.5 | convolution fusion | flops 8589934592 | bytes 20971524 | tf_op jit(solution)/shard_map/dot_general | solution.py:163
  289.9 0.0 collective-permute-done.3
  289.9 0.0 copy-done.1
  289.9 8.4 %add_add_fusion = f32[1024,1024]{0,1:T(8,128)S(1)} fusion(f32[1024,1024]{0,1:T(8,128)} %fusion.14, f32[1024,1024]{0,1:T(8,128)S(1)} %fusion.16, f32[1024,1024]{0,1:T(8,128)} %fusion.3, f32[1024,1024]{0,1:T(8,128)S(1)} %fusion.18, f32[1024]{0:T(1024)S(1)} %copy-done.1, bf16[1024,1024]{1,0:T(8,128)(2,1)} %collective-permute-done.3, ...), kind=kOutput, calls=%fused_computation.17 | convolution fusion | flops 2152726528 | bytes 25169924 | tf_op jit(solution)/shard_map/dot_general | solution.py:163
  298.3 1.7 fusion.56
  300.0 3.8 %copy.34 = f32[1024,8,64]{2,1,0:T(8,128)} copy(f32[1024,8,64]{0,2,1:T(8,128)} %get-tuple-element.12) | data formatting | bytes 4194304
  303.8 2.8 copy.35
  306.6 4.0 %subtract_convert_fusion = (bf16[1024,8,64]{2,1,0:T(8,128)(2,1)S(1)}, bf16[1024,8,64]{2,1,0:T(8,128)(2,1)S(1)}) fusion(f32[1024,8,64]{2,1,0:T(8,128)} %copy.35, f32[1024,8,64]{2,1,0:T(8,128)} %copy.34, f32[1024,64]{1,0:T(8,128)S(1)} %get-tuple-element.22, f32[1024,64]{1,0:T(8,128)S(1)} %get-tuple-element.21), kind=kLoop, calls=%fused_computation.16 | loop fusion | flops 4194304 | bytes 6815744 | tf_op jit(solution)/shard_map/convert.4
  310.7 0.0 copy-start.7
  310.7 1.2 pad_maximum_fusion
  311.8 1.9 copy.38
  313.8 0.0 copy-done.7
  313.8 8.2 %fusion.57 = f32[1024,256]{1,0:T(8,128)S(1)} fusion(bf16[1024,8192]{1,0:T(8,128)(2,1)} %all-gather.4.cloned.1.call-done, bf16[8192,256]{1,0:T(8,128)(2,1)S(1)} %copy-done.7), kind=kOutput, calls=%fused_computation.100 | convolution fusion | flops 4294967296 | bytes 22020096 | tf_op jit(solution)/shard_map/dot_general | solution.py:229
  322.0 0.1 fusion.31
  322.0 2.4 fusion.27
  324.5 1.0 maximum_bitcast_fusion.kvc_ref
  325.5 46.0 %shard_map.109 = bf16[1024,1024]{1,0:T(8,128)(2,1)} custom-call(s32[4]{0:T(128)} %get-tuple-element.6.prefix_ref, s32[4]{0:T(128)} %get-tuple-element.5.length_ref, s32[4]{0:T(128)} %and_select_fusion.offset_ref, bf16[1024,1024]{1,0:T(8,128)(2,1)} %bitcast.26, bf16[1536,256]{1,0:T(8,128)(2,1)} %bitcast.27, bf16[1024,256]{1,0:T(8,128)(2,1)} %maximum_bitcast_fusion.kvc_ref), custom_call_target="tpu_custom_call" | custom-call | flops 7516192768 | bytes 4194304 | tf_op jit(solution)/shard_map/pallas_call | solution.py:115
  (9 shorter events, 0.1 us)
Async XLA Ops:
  6.5 3.4 copy-start.6
  6.5 3.4 copy-start
  6.5 154.1 %all-gather.6.cloned.1.call-start = ((), (), s32[]{:S(2)}) async-start(), calls=%async_computation.1 | async-start | bytes 6291456 | tf_op jit(solution)/shard_map/all_gather | solution.py:213
  9.8 249.0 %all-gather.4.cloned.1.call-start = ((), (), s32[]{:S(2)}) async-start(), calls=%async_computation | async-start | bytes 18874368 | tf_op jit(solution)/shard_map/all_gather | solution.py:207
  30.4 6.7 %copy-start.2 = (s32[16]{0:T(128)S(1)}, s32[16]{0:T(128)}, u32[]{:S(2)}) copy-start(s32[16]{0:T(128)} %param.21) | copy-start | bytes 196
  30.4 6.7 %copy-start.5 = (s32[16]{0:T(128)S(1)}, s32[16]{0:T(128)}, u32[]{:S(2)}) copy-start(s32[16]{0:T(128)} %param.20) | copy-start | bytes 196
  34.4 81.1 %collective-permute-start = (bf16[1024,1024]{1,0:T(8,128)(2,1)}, bf16[1024,1024]{1,0:T(8,128)(2,1)}, u32[]{:S(2)}, u32[]{:S(2)}) collective-permute-start(bf16[1024,1024]{1,0:T(8,128)(2,1)} %get-tuple-element.10), channel_id=1, source_target_pairs={{0,16},{16,0},{1,17},{17,1},{2,18},{18,2},{3,19},{19,3},{4,20},{20... | collective-permute-start | bytes 6291464 | tf_op jit(solution)/shard_map/ppermute | solution.py:154
  36.0 123.2 %collective-permute-start.1 = (bf16[1024,1024]{1,0:T(8,128)(2,1)S(1)}, bf16[1024,1024]{1,0:T(8,128)(2,1)}, u32[]{:S(2)}, u32[]{:S(2)}) collective-permute-start(bf16[1024,1024]{1,0:T(8,128)(2,1)S(1)} %get-tuple-element.9), channel_id=1, source_target_pairs={{0,16},{16,0},{1,17},{17,1},{2,18},{18,2},{3,19},{19,3},{4,20},{20... | collective-permute-start | bytes 6291464 | tf_op jit(solution)/shard_map/ppermute | solution.py:154
  44.0 122.6 %copy-start.3 = (f32[128]{0:T(128)S(1)}, f32[128]{0:T(128)}, u32[]{:S(2)}) copy-start(f32[128]{0:T(128)} %param.18) | copy-start | bytes 1540
  44.0 122.6 %copy-start.4 = (f32[128]{0:T(128)S(1)}, f32[128]{0:T(128)}, u32[]{:S(2)}) copy-start(f32[128]{0:T(128)} %param.19) | copy-start | bytes 1540
  115.5 152.7 %collective-permute-start.2 = (bf16[1024,1024]{1,0:T(8,128)(2,1)}, bf16[1024,1024]{1,0:T(8,128)(2,1)}, u32[]{:S(2)}, u32[]{:S(2)}) collective-permute-start(bf16[1024,1024]{1,0:T(8,128)(2,1)} %collective-permute-done), channel_id=1, source_target_pairs={{0,1},{1,0},{2,3},{3,2},{4,5},{5,4},{6,7},{7,6},{8,9},{9,8},{10,11... | collective-permute-start | bytes 6291464 | tf_op jit(solution)/shard_map/ppermute | solution.py:159
  159.2 130.7 %collective-permute-start.3 = (bf16[1024,1024]{1,0:T(8,128)(2,1)}, bf16[1024,1024]{1,0:T(8,128)(2,1)}, u32[]{:S(2)}, u32[]{:S(2)}) collective-permute-start(bf16[1024,1024]{1,0:T(8,128)(2,1)} %collective-permute-done.1), channel_id=1, source_target_pairs={{0,1},{1,0},{2,3},{3,2},{4,5},{5,4},{6,7},{7,6},{8,9},{9,8},{10,11... | collective-permute-start | bytes 6291464 | tf_op jit(solution)/shard_map/ppermute | solution.py:159
  274.8 15.1 %copy-start.1 = (f32[1024]{0:T(1024)S(1)}, f32[1024]{0:T(1024)}, u32[]{:S(2)}) copy-start(f32[1024]{0:T(1024)} %param.17) | copy-start | bytes 12292
  310.7 3.1 copy-start.7
Sparse Core Ops, SparseCore 0:
  10.0 93.2 all-gather.5
  104.9 153.8 all-gather.3

commit v2 on v1

--- a/solution.py
+++ b/solution.py
@@ -210,7 +210,15 @@
     cand_pos = prefix_row + row_ids % CLEN
     prompt_pos = joined * prompt_dev + jnp.arange(prompt_dev, dtype=jnp.int32)
     key_value = jnp.concatenate([w_key, w_value], axis=1)
-    key_value = lax.all_gather(key_value, "cache", axis=0, tiled=True)
+    if lax.axis_size("cache") == 2:
+        other_half = lax.ppermute(key_value, "cache", [(0, 1), (1, 0)])
+        key_value = jnp.where(
+            lax.axis_index("cache") == 0,
+            jnp.concatenate([key_value, other_half], axis=0),
+            jnp.concatenate([other_half, key_value], axis=0),
+        )
+    else:
+        key_value = lax.all_gather(key_value, "cache", axis=0, tiled=True)
     kv_prompt = jnp.dot(normed_p, key_value, preferred_element_type=jnp.float32)
 
     def keys_values(product, positions):

time: 382 us -> 355 us (0.929)
  waiting for transfers between devices: 159 us -> 119 us
  matrix products: 53.5 us -> 60.6 us
  Pallas kernels: 46 us -> 52.6 us
    all_gather x1, waiting for transfers between devices: 45.1 us -> 0.01 us  [per_device(): normed_c = lax.all_gather(normed_part, 'tp', axis=1, tiled=True)]
    ppermute x0 -> x1, waiting for transfers between devices: none -> 39 us  [per_device(): other_half = lax.ppermute(key_value, 'cache', [(0, 1), (1, 0)])]
    ppermute x2, waiting for transfers between devices: 114 us -> 80.2 us  [query_product(): lax.ppermute(lax.dynamic_slice_in_dim(w_query, (2 * side + turn) * part,...]
    pallas_call x1, Pallas kernels: 46 us -> 52.6 us  [attend(): pl.pallas_call(functools.partial(attend_kernel, heads=heads, chunk=chunk,...]
    dot_general x1, matrix products: 8.16 us -> 12.8 us  [per_device(): jnp.dot(normed_c, key_value, preferred_element_type=jnp.float32)]
    unnamed x19 -> x20, local copies, waits for them, and re-layouts: 8.61 us -> 9.69 us
  transfers between devices with their start and end apart: 6 -> 6, of which waited for: 3 -> 2; matrix products, arithmetic and copies ran while one was open for 14% -> 15% of each run, Pallas kernels for 0% -> 0%
where the time goes in v2:
time: 355 us; the launch traced here: 354 us
  waiting for transfers between devices  119 us (34%)
  blocking collectives  62.4 us (18%)
  matrix products  60.6 us (17%)
  Pallas kernels  52.6 us (15%)
  other arithmetic  23.1 us (7%)
  local copies, waits for them, and re-layouts  17.4 us (5%)
  between operations  13.6 us (4%)
  starting transfers between devices  5.57 us (2%)
    ppermute x2, waiting for transfers between devices, query_product(): lax.ppermute(lax.dynamic_slice_in_dim(w_query, (2 * side + turn) * part,...  80.2 us
    pallas_call x1, Pallas kernels, attend(): pl.pallas_call(functools.partial(attend_kernel, heads=heads, chunk=chunk,...  52.6 us
    all_gather x1, blocking collectives, per_device(): lax.all_gather(keys_values(kv_prompt, prompt_pos), ('cache', 'cand'), axi...  44.3 us
    dot_general x5, matrix products, product(): return jnp.dot(columns, weights, preferred_element_type=jnp.float32)  39.4 us
    ppermute x1, waiting for transfers between devices, per_device(): other_half = lax.ppermute(key_value, 'cache', [(0, 1), (1, 0)])  39 us
    psum x1, blocking collectives, per_device(): squares = lax.psum(jnp.sum(widened_c * widened_c, axis=-1), 'tp')  18.1 us
    dot_general x1, matrix products, per_device(): jnp.dot(normed_c, key_value, preferred_element_type=jnp.float32)  12.8 us
    unnamed x20, local copies, waits for them, and re-layouts  9.69 us
  transfers between devices with their start and end apart: 6, of which 2 were waited for; matrix products, arithmetic and copies ran while one was open for 15% of the time, Pallas kernels for 0%

profile of v2, /device:TPU:0, one launch (start us, length us, event | category | flops | bytes accessed | tf_op | source)
XLA Modules:
  0.0 354.3 jit_solution(3920293849003582764)
XLA Ops:
  6.5 0.0 all-gather.3.cloned.1.call-start
  6.5 2.1 fusion.9
  8.6 18.1 %psum.7 = f32[1024]{0:T(1024)S(1)} all-reduce(f32[1024]{0:T(1024)S(1)} %fusion.9), channel_id=1, replica_groups=mesh['cache'=2,'tp'=8,'cand'=2] {'tp'}, use_global_device_ids=true, to_apply=%region_3.4 | all-reduce | flops 1024 | bytes 8192 | tf_op jit(solution)/shard_map/psum | solution.py:201
  26.7 0.7 dynamic_slice.24
  27.4 3.5 fusion.11
  30.9 0.0 all-gather.3.cloned.1.call-update
  30.9 0.0 copy-start
  30.9 0.0 copy-start.1
  31.0 4.1 %constant_dynamic-slice_fusion = (bf16[1024,1024]{1,0:T(8,128)(2,1)S(1)}, bf16[1024,1024]{1,0:T(8,128)(2,1)}) fusion(bf16[4096,1024]{1,0:T(8,128)(2,1)} %param.14, s32[]{:T(128)S(6)} %select_n.88, s32[]{:T(128)S(6)} %select_n.86), kind=kLoop, calls=%fused_computation.92 | loop fusion | bytes 8388616 | tf_op jit(solution)/shard_map/dynamic_slice | solution.py:155
  35.1 0.0 copy-start.3
  35.1 0.0 copy-start.6
  35.1 1.5 collective-permute-start.1
  36.6 0.5 collective-permute-start
  37.1 0.0 copy-done
  37.1 1.1 constant_dynamic-update-slice_fusion.1
  38.2 0.0 copy-done.1
  38.2 1.1 constant_dynamic-update-slice_fusion
  39.3 0.0 copy-start.7
  39.3 1.5 collective-permute-start.4
  40.9 0.6 and_select_fusion.offset_ref
  41.5 0.0 copy-done.3
  41.5 0.0 copy-done.6
  41.5 0.8 select_reduce_fusion.1
  42.3 0.1 select_reduce_fusion
  42.3 4.2 %fusion = f32[384]{0:T(512)S(1)} fusion(bf16[384,8192]{1,0:T(8,128)(2,1)} %param.11), kind=kLoop, calls=%fused_computation.2 | loop fusion | flops 9436800 | bytes 6292992 | tf_op jit(solution)/shard_map/reduce_sum | solution.py:197
  46.5 1.9 multiply_cosine_fusion.1
  48.4 0.0 copy-start.4
  48.4 0.0 copy-start.5
  48.5 80.2 %collective-permute-done = bf16[1024,1024]{1,0:T(8,128)(2,1)} collective-permute-done((bf16[1024,1024]{1,0:T(8,128)(2,1)}, bf16[1024,1024]{1,0:T(8,128)(2,1)}, u32[]{:S(2)}, u32[]{:S(2)}) %collective-permute-start) | collective-permute-done | bytes 2097184 | tf_op jit(solution)/shard_map/ppermute | solution.py:154
  128.6 1.5 collective-permute-start.2
  130.1 0.0 collective-permute-done.1
  130.1 0.5 collective-permute-start.3
  130.7 39.0 %collective-permute-done.4 = bf16[4096,256]{1,0:T(8,128)(2,1)} collective-permute-done((bf16[4096,256]{1,0:T(8,128)(2,1)}, bf16[4096,256]{1,0:T(8,128)(2,1)}, u32[]{:S(2)}, u32[]{:S(2)}) %collective-permute-start.4) | collective-permute-done | bytes 2097184 | tf_op jit(solution)/shard_map/ppermute | solution.py:214
  169.6 0.0 copy-done.7
  169.6 8.4 %fusion.5 = f32[384,256]{1,0:T(8,128)S(1)} fusion(bf16[384,8192]{1,0:T(8,128)(2,1)} %param.11, f32[8192]{0:T(1024)S(1)} %copy-done.7, f32[384]{0:T(512)S(1)} %add_rsqrt_fusion.1, bf16[4096,256]{1,0:T(8,128)(2,1)} %collective-permute-done.4, bf16[4096,256]{1,0:T(8,128)(2,1)} %constant_dynamic-update-slice_fusion, pred[]{:T(512)S(6)} %eq.23), kind=kOutput, calls=%fused_computation.7 | convolution fusion | flops 1642070016 | bytes 10913281 | tf_op jit(solution)/shard_map/dot_general | solution.py:222
  178.0 0.0 copy-done.4
  178.1 0.0 copy-done.5
  178.1 0.8 fusion.39
  178.9 0.1 pad_maximum_fusion.1
  179.1 44.3 %all-gather = bf16[1536,1,256]{2,0,1:T(8,128)(2,1)} all-gather(bf16[384,1,256]{2,0,1:T(8,128)(2,1)S(1)} %pad_maximum_fusion.1), channel_id=2, replica_groups=mesh['cache'=2,'tp'=8,'cand'=2] {'cache','cand'}, dimensions={0}, use_global_device_ids=true | all-gather | bytes 983040 | tf_op jit(solution)/shard_map/all_gather | solution.py:233
  223.3 0.0 all-gather.3.cloned.1.call-done
  223.3 4.7 %fusion.16 = f32[1024,1024]{0,1:T(8,128)S(1)} fusion(bf16[1024,1024]{1,0:T(8,128)(2,1)} %collective-permute-done.1, bf16[1024,8192]{1,0:T(8,128)(2,1)} %all-gather.3.cloned.1.call-done, s32[]{:T(128)S(6)} %select_n.87), kind=kOutput, calls=%fused_computation.25 | convolution fusion | flops 2147483648 | bytes 8388612 | tf_op jit(solution)/shard_map/dot_general | solution.py:163
  228.0 4.7 %fusion.18 = f32[1024,1024]{0,1:T(8,128)S(1)} fusion(bf16[1024,1024]{1,0:T(8,128)(2,1)} %collective-permute-done, bf16[1024,8192]{1,0:T(8,128)(2,1)} %all-gather.3.cloned.1.call-done, s32[]{:T(128)S(6)} %select_n.85), kind=kOutput, calls=%fused_computation.27 | convolution fusion | flops 2147483648 | bytes 8388612 | tf_op jit(solution)/shard_map/dot_general | solution.py:163
  232.8 0.0 collective-permute-done.2
  232.8 6.6 %fusion.14 = f32[1024,1024]{0,1:T(8,128)} fusion(bf16[1024,1024]{1,0:T(8,128)(2,1)} %collective-permute-done.2, bf16[1024,8192]{1,0:T(8,128)(2,1)} %all-gather.3.cloned.1.call-done, s32[]{:T(128)S(6)} %select_n.89), kind=kOutput, calls=%fused_computation.23 | convolution fusion | flops 2147483648 | bytes 8388612 | tf_op jit(solution)/shard_map/dot_general | solution.py:163
  239.3 0.0 copy-start.2
  239.3 15.1 %fusion.3 = f32[1024,1024]{0,1:T(8,128)} fusion(bf16[4096,1024]{1,0:T(8,128)(2,1)} %param.14, bf16[1024,8192]{1,0:T(8,128)(2,1)} %all-gather.3.cloned.1.call-done, s32[]{:T(128)S(6)} %select_n.84), kind=kOutput, calls=%fused_computation.5 | convolution fusion | flops 8589934592 | bytes 20971524 | tf_op jit(solution)/shard_map/dot_general | solution.py:163
  254.4 0.0 collective-permute-done.3
  254.4 0.0 copy-done.2
  254.4 8.4 %add_add_fusion = f32[1024,1024]{0,1:T(8,128)S(1)} fusion(f32[1024,1024]{0,1:T(8,128)} %fusion.14, f32[1024,1024]{0,1:T(8,128)S(1)} %fusion.16, f32[1024,1024]{0,1:T(8,128)} %fusion.3, f32[1024,1024]{0,1:T(8,128)S(1)} %fusion.18, f32[1024]{0:T(1024)S(1)} %copy-done.2, bf16[1024,1024]{1,0:T(8,128)(2,1)} %collective-permute-done.3, ...), kind=kOutput, calls=%fused_computation.18 | convolution fusion | flops 2152726528 | bytes 25169924 | tf_op jit(solution)/shard_map/dot_general | solution.py:163
  262.8 1.7 fusion.59
  264.6 3.9 %copy.34 = f32[1024,8,64]{2,1,0:T(8,128)} copy(f32[1024,8,64]{0,2,1:T(8,128)} %get-tuple-element.12) | data formatting | bytes 4194304
  268.4 2.7 copy.35
  271.2 4.3 %subtract_convert_fusion = (bf16[1024,8,64]{2,1,0:T(8,128)(2,1)S(1)}, bf16[1024,8,64]{2,1,0:T(8,128)(2,1)S(1)}) fusion(f32[1024,8,64]{2,1,0:T(8,128)} %copy.35, f32[1024,8,64]{2,1,0:T(8,128)} %copy.34, f32[1024,64]{1,0:T(8,128)S(1)} %get-tuple-element.22, f32[1024,64]{1,0:T(8,128)S(1)} %get-tuple-element.21), kind=kLoop, calls=%fused_computation.17 | loop fusion | flops 4194304 | bytes 6815744 | tf_op jit(solution)/shard_map/convert.4
  275.4 1.2 pad_maximum_fusion
  276.6 2.0 copy.38
  278.6 12.8 %fusion.26 = f32[1024,256]{1,0:T(8,128)S(1)} fusion(bf16[1024,8192]{1,0:T(8,128)(2,1)} %all-gather.3.cloned.1.call-done, bf16[4096,256]{1,0:T(8,128)(2,1)} %collective-permute-done.4, bf16[4096,256]{1,0:T(8,128)(2,1)} %constant_dynamic-update-slice_fusion, pred[]{:T(512)S(6)} %eq.23), kind=kOutput, calls=%fused_computation.37 | convolution fusion | flops 4313841664 | bytes 22020096 | tf_op jit(solution)/shard_map/dot_general | solution.py:237
  291.4 0.1 fusion.32
  291.4 2.4 fusion.28
  293.9 1.0 maximum_bitcast_fusion.kvc_ref
  294.9 52.6 %shard_map.109 = bf16[1024,1024]{1,0:T(8,128)(2,1)} custom-call(s32[4]{0:T(128)} %get-tuple-element.6.prefix_ref, s32[4]{0:T(128)} %get-tuple-element.5.length_ref, s32[4]{0:T(128)} %and_select_fusion.offset_ref, bf16[1024,1024]{1,0:T(8,128)(2,1)} %bitcast.24, bf16[1536,256]{1,0:T(8,128)(2,1)} %bitcast.25, bf16[1024,256]{1,0:T(8,128)(2,1)} %maximum_bitcast_fusion.kvc_ref), custom_call_target="tpu_custom_call" | custom-call | flops 7516192768 | bytes 4194304 | tf_op jit(solution)/shard_map/pallas_call | solution.py:115
  (8 shorter events, 0.1 us)
Async XLA Ops:
  6.5 216.8 %all-gather.3.cloned.1.call-start = ((), (), s32[]{:S(2)}) async-start(), calls=%async_computation | async-start | bytes 18874368 | tf_op jit(solution)/shard_map/all_gather | solution.py:207
  30.9 6.2 %copy-start = (bf16[4096,128]{1,0:T(8,128)(2,1)S(1)}, bf16[4096,128]{1,0:T(8,128)(2,1)}, u32[]{:S(2)}) copy-start(bf16[4096,128]{1,0:T(8,128)(2,1)} %param.15) | copy-start | bytes 3145732
  30.9 7.3 %copy-start.1 = (bf16[4096,128]{1,0:T(8,128)(2,1)S(1)}, bf16[4096,128]{1,0:T(8,128)(2,1)}, u32[]{:S(2)}) copy-start(bf16[4096,128]{1,0:T(8,128)(2,1)} %param.16) | copy-start | bytes 3145732
  35.1 6.4 %copy-start.3 = (s32[16]{0:T(128)S(1)}, s32[16]{0:T(128)}, u32[]{:S(2)}) copy-start(s32[16]{0:T(128)} %param.21) | copy-start | bytes 196
  35.1 6.4 %copy-start.6 = (s32[16]{0:T(128)S(1)}, s32[16]{0:T(128)}, u32[]{:S(2)}) copy-start(s32[16]{0:T(128)} %param.20) | copy-start | bytes 196
  35.1 95.0 %collective-permute-start.1 = (bf16[1024,1024]{1,0:T(8,128)(2,1)S(1)}, bf16[1024,1024]{1,0:T(8,128)(2,1)}, u32[]{:S(2)}, u32[]{:S(2)}) collective-permute-start(bf16[1024,1024]{1,0:T(8,128)(2,1)S(1)} %get-tuple-element.9), channel_id=1, source_target_pairs={{0,16},{16,0},{1,17},{17,1},{2,18},{18,2},{3,19},{19,3},{4,20},{20... | collective-permute-start | bytes 6291464 | tf_op jit(solution)/shard_map/ppermute | solution.py:154
  36.6 92.0 %collective-permute-start = (bf16[1024,1024]{1,0:T(8,128)(2,1)}, bf16[1024,1024]{1,0:T(8,128)(2,1)}, u32[]{:S(2)}, u32[]{:S(2)}) collective-permute-start(bf16[1024,1024]{1,0:T(8,128)(2,1)} %get-tuple-element.10), channel_id=1, source_target_pairs={{0,16},{16,0},{1,17},{17,1},{2,18},{18,2},{3,19},{19,3},{4,20},{20... | collective-permute-start | bytes 6291464 | tf_op jit(solution)/shard_map/ppermute | solution.py:154
  39.3 130.3 %copy-start.7 = (f32[8192]{0:T(1024)S(1)}, f32[8192]{0:T(1024)}, u32[]{:S(2)}) copy-start(f32[8192]{0:T(1024)} %param.13) | copy-start | bytes 98308
  39.3 130.3 %collective-permute-start.4 = (bf16[4096,256]{1,0:T(8,128)(2,1)}, bf16[4096,256]{1,0:T(8,128)(2,1)}, u32[]{:S(2)}, u32[]{:S(2)}) collective-permute-start(bf16[4096,256]{1,0:T(8,128)(2,1)} %constant_dynamic-update-slice_fusion), channel_id=1, source_target_pairs={{0,16},{16,0},{1,17},{17,1},{2,18},{18,2},{3,19},{19,3},{4,20},{20... | collective-permute-start | bytes 6291464 | tf_op jit(solution)/shard_map/ppermute | solution.py:214
  48.4 129.6 %copy-start.4 = (f32[128]{0:T(128)S(1)}, f32[128]{0:T(128)}, u32[]{:S(2)}) copy-start(f32[128]{0:T(128)} %param.18) | copy-start | bytes 1540
  48.4 129.6 %copy-start.5 = (f32[128]{0:T(128)S(1)}, f32[128]{0:T(128)}, u32[]{:S(2)}) copy-start(f32[128]{0:T(128)} %param.19) | copy-start | bytes 1540
  128.6 104.1 %collective-permute-start.2 = (bf16[1024,1024]{1,0:T(8,128)(2,1)}, bf16[1024,1024]{1,0:T(8,128)(2,1)}, u32[]{:S(2)}, u32[]{:S(2)}) collective-permute-start(bf16[1024,1024]{1,0:T(8,128)(2,1)} %collective-permute-done), channel_id=1, source_target_pairs={{0,1},{1,0},{2,3},{3,2},{4,5},{5,4},{6,7},{7,6},{8,9},{9,8},{10,11... | collective-permute-start | bytes 6291464 | tf_op jit(solution)/shard_map/ppermute | solution.py:159
  130.1 124.3 %collective-permute-start.3 = (bf16[1024,1024]{1,0:T(8,128)(2,1)}, bf16[1024,1024]{1,0:T(8,128)(2,1)}, u32[]{:S(2)}, u32[]{:S(2)}) collective-permute-start(bf16[1024,1024]{1,0:T(8,128)(2,1)} %collective-permute-done.1), channel_id=1, source_target_pairs={{0,1},{1,0},{2,3},{3,2},{4,5},{5,4},{6,7},{7,6},{8,9},{9,8},{10,11... | collective-permute-start | bytes 6291464 | tf_op jit(solution)/shard_map/ppermute | solution.py:159
  239.3 15.1 %copy-start.2 = (f32[1024]{0:T(1024)S(1)}, f32[1024]{0:T(1024)}, u32[]{:S(2)}) copy-start(f32[1024]{0:T(1024)} %param.17) | copy-start | bytes 12292
Sparse Core Ops, SparseCore 0:
  31.0 149.2 all-gather.2
